TPU v7x, 32 devices: a whole 2x2x4 slice. The times are simulated.
32 devices in a mesh: dp: 8 (over z, x), wshard: 4 (over y, core).
Axes of the slice: x: 2, y: 2, z: 4, core: 2. Of those that a mesh axis runs over, the one named last changes fastest.
Arguments:
- tokens: bfloat16 [16384, 1024], P(('dp', 'wshard')), may hold values from -6 to 6
- cotangent: bfloat16 [16384, 1024], P(('dp', 'wshard')), may hold values from -6 to 6
- span_starts: int32 [32], P(('dp', 'wshard')), may hold values from 0 to 256
- routes: int32 [16384, 2], P(('dp', 'wshard')), may hold values from 0 to 7, all different within a row; in each aligned block of 512 rows (0 to 511, 512 to 1023, ...) at most 160 rows name the same one
- norm_gains: float32 [2, 1024], replicated, may hold values from 0.5 to 1.5
- bias_table: float32 [32, 16], replicated, may hold values from -4 to 4
- router: bfloat16 [1024, 8], replicated, may hold values from -0.1875 to 0.1875
- attn_qkv: bfloat16 [3, 1024, 1024], P(None, None, 'wshard'), may hold values from -0.1875 to 0.1875
- attn_out: bfloat16 [1024, 1024], P(None, 'wshard'), may hold values from -1.5 to 1.5
- expert_in: bfloat16 [8, 2, 1024, 2816], P('dp', None, None, 'wshard'), may hold values from -0.1875 to 0.1875
- expert_down: bfloat16 [8, 2816, 1024], P('dp', 'wshard'), may hold values from -0.109375 to 0.109375
Outputs:
- output: bfloat16 [16384, 1024], P(('dp', 'wshard'))
- grad_tokens: bfloat16 [16384, 1024], P(('dp', 'wshard'))
- grad_norm_gains: float32 [2, 1024], replicated
- grad_bias_table: float32 [32, 16], replicated
- grad_router: float32 [1024, 8], replicated
- grad_attn_qkv: float32 [3, 1024, 1024], P(None, None, 'wshard')
- grad_attn_out: float32 [1024, 1024], P(None, 'wshard')
- grad_expert_in: float32 [8, 2, 1024, 2816], P('dp', None, None, 'wshard')
- grad_expert_down: float32 [8, 2816, 1024], P('dp', 'wshard')
Inputs may be any that keep to these rules, and one draw needn't show every extreme that they name: `routes`: each token names two different experts; among the rows of one device no expert is named more than 160 times, a bound that some block reaches. `span_starts`: the picture span of a sequence covers 256 positions inside it.
All inputs are finite; a program needn't handle non-finite values.
Results may differ from a plain program's by a relative error of at most 0.015.
The roundings to bfloat16 on the way count: a program that leaves them out, or rounds other values in their place, can miss the bound.
Values may be sent and summed in bfloat16 or wider, within the bound.
A program may use at most 256 MiB of HBM per device.

v0:
```python
import functools

import jax
import jax.numpy as jnp
import numpy as np
from jax import lax
from jax.experimental import pallas as pl
from jax.experimental.pallas import tpu as pltpu
from jax.sharding import PartitionSpec as P

PIC = 256
PRECISE = lax.Precision.HIGHEST
EPSILON = 1e-06
MASKED_SCORE = -1e30
BUCKET_EDGES = (8, 11, 16, 23, 32, 45, 64, 91)
TILE = 128
F32 = jnp.float32
BF16 = jnp.bfloat16
I32 = jnp.int32
VMEM = pl.BlockSpec(memory_space=pltpu.VMEM)
SMEM = pl.BlockSpec(memory_space=pltpu.SMEM)
ANY = pl.BlockSpec(memory_space=pl.ANY)
LIGHT = 1024
EXTRA = 8


def dot_nn(a, b):
    return lax.dot_general(a, b, (((1,), (0,)), ((), ())), preferred_element_type=F32)


def dot_nt(a, b):
    return lax.dot_general(a, b, (((1,), (1,)), ((), ())), preferred_element_type=F32)


def dot_tn(a, b):
    return lax.dot_general(a, b, (((0,), (0,)), ((), ())), preferred_element_type=F32)


def iota(shape, axis):
    return lax.broadcasted_iota(I32, shape, axis)


def shape_of(shape, dtype):
    return jax.ShapeDtypeStruct(shape, dtype)


def call(body, out, args, specs, scratch=(), name=None):
    return pl.pallas_call(
        body,
        out_shape=out,
        in_specs=specs,
        out_specs=jax.tree.map(lambda _: VMEM, out),
        scratch_shapes=list(scratch),
        cost_estimate=pl.CostEstimate(flops=LIGHT, bytes_accessed=LIGHT, transcendentals=0),
        name=name,
    )(*args)


def bucket_of(offset):
    magnitude = np.abs(offset)
    coarse = 7 + sum((magnitude >= bound).astype(np.int32) for bound in BUCKET_EDGES)
    return np.where(magnitude < 8, magnitude, coarse) + 16 * (offset < 0)


def diagonal_ones(bucket_count):
    column = np.arange(2 * TILE)
    signed = np.where(column < TILE, column, column - 2 * TILE)
    offsets = np.concatenate([TILE * step - signed for step in (-1, 0, 1)])
    used = np.tile(column != TILE, 3)
    hit = bucket_of(offsets)[None, :] == np.arange(bucket_count)[:, None]
    near = (hit & used[None, :]).astype(np.float32)
    far = np.zeros((bucket_count, 2 * TILE), np.float32)
    far[bucket_of(np.array(TILE)), :TILE] = 1
    far[bucket_of(np.array(-TILE)), TILE:] = 1
    return np.concatenate([near, far], 1)


def onehot_rows(first, count, slots_row):
    index = iota((count, slots_row.shape[1]), 0) + first
    hit = (index == slots_row[0:1, :]) | (index == slots_row[1:2, :])
    return hit.astype(F32).astype(BF16)


def onehot_columns(slots_column, first, count):
    index = iota((slots_column.shape[0], count), 1) + first
    return index == slots_column


def route_slots(experts, capacity, routes):
    tokens = routes.shape[1]
    label = iota((experts, tokens), 0)
    hits = ((routes[0:1] == label) | (routes[1:2] == label)).astype(F32).astype(BF16)
    earlier = iota((tokens, tokens), 0) < iota((tokens, tokens), 1)
    before = dot_nn(hits, earlier.astype(F32).astype(BF16))
    slots = []
    for k in range(2):
        own = jnp.sum(jnp.where(routes[k : k + 1] == label, before, 0.0), 0, keepdims=True)
        slots.append(own.astype(I32) + routes[k : k + 1] * capacity)
    return jnp.concatenate(slots * 4, 0)


def unit_norm(values):
    recip = lax.rsqrt(jnp.mean(values * values, -1, keepdims=True) + EPSILON)
    return values * recip, recip


def fill_mask(mask_ref, span_start):
    size = mask_ref.shape[0]
    i, j = iota((size, size), 0), iota((size, size), 1)

    def inside(p):
        return (p >= span_start) & (p < span_start + PIC)

    visible = (j <= i) | (inside(i) & inside(j))
    mask_ref[...] = jnp.where(visible, 0.0, MASKED_SCORE)


def head_lanes(which, size):
    lane = iota((1, 2 * size), 1)
    return ((lane >= size) == (which == 1)).astype(F32).astype(BF16)


def spread_bias(table_ref, ones_ref):
    pieces = [dot_nn(piece.astype(BF16), ones_ref[...]) for piece in split_three(table_ref[...])]
    return pieces[0] + pieces[1] + pieces[2]


def bias_tiles(diag_row):
    tiles = []
    for step in range(3):
        row = diag_row[:, 2 * TILE * step : 2 * TILE * (step + 1)]
        wide = jnp.broadcast_to(row, (TILE, 2 * TILE))
        tiles.append(pltpu.roll(wide, 0, 1, stride=1, stride_axis=0)[:, :TILE])
    return tiles, (diag_row[:, 6 * TILE : 7 * TILE], diag_row[:, 7 * TILE :])


def score_tiles(block, query, keys, tiles, far, mask_ref):
    raw = dot_nt(query, keys)
    rows = slice(block * TILE, (block + 1) * TILE)
    result = []
    for other in range(keys.shape[0] // TILE):
        piece = raw[:, other * TILE : (other + 1) * TILE]
        step = block - other
        piece = piece + (far[0] if step >= 2 else far[1] if step <= -2 else tiles[step + 1])
        if step <= 0:
            piece = piece + mask_ref[rows, other * TILE : (other + 1) * TILE]
        result.append(piece)
    return result


def softmax_tiles(pieces):
    top = functools.reduce(jnp.maximum, pieces)
    top = jnp.max(top, -1, keepdims=True)
    powers = [jnp.exp(piece - top) for piece in pieces]
    total = jnp.sum(functools.reduce(jnp.add, powers), -1, keepdims=True)
    scale = 1.0 / total
    return [power * scale for power in powers]


def split_three(value):
    high = value.astype(BF16).astype(F32)
    middle = (value - high).astype(BF16).astype(F32)
    return high, middle, value - high - middle


def remote_copy(source, target, sent, got, axis, peer):
    return pltpu.make_async_remote_copy(
        src_ref=source,
        dst_ref=target,
        send_sem=sent,
        recv_sem=got,
        device_id={axis: peer},
        device_id_type=pl.DeviceIdType.MESH,
    )


def turns_of(size):
    half, quarter = size // 2, size // 4
    return range(half, half + quarter), range(half + quarter, size), range(1, half)


def greet(peers):
    barrier = pltpu.get_barrier_semaphore()
    for axis, peer in peers:
        pl.semaphore_signal(
            barrier, inc=1, device_id={axis: peer}, device_id_type=pl.DeviceIdType.MESH
        )
    pl.semaphore_wait(barrier, len(peers))


def project_and_attend(place, group, groups, head_size, norm, diag_ref, w_ref, qkv_ref, mix_ref, mask):
    count = norm.shape[0]
    cols = w_ref.shape[-1]
    width = 2 * head_size
    owner = flip(place, group, groups)
    for c in range(3):
        qkv_ref[group, c] = dot_nn(norm[...], w_ref[group, c]).astype(BF16)

    def pair(p, carry):
        offset = pl.multiple_of(p * width, width)
        lanes = pl.ds(offset, width)
        query, keys, value = (qkv_ref[group, c, :, lanes] for c in range(3))
        mixed = [None] * (count // TILE)
        for which in range(2):
            head = owner * (cols // head_size) + 2 * p + which
            own = head_lanes(which, head_size)
            own_query, own_value = query * (own * 0.125), value * own
            tiles, far = bias_tiles(diag_ref[pl.ds(head, 1), :])
            for block in range(count // TILE):
                rows = slice(block * TILE, (block + 1) * TILE)
                pieces = score_tiles(block, own_query[rows], keys, tiles, far, mask)
                probs = jnp.concatenate([t.astype(BF16) for t in softmax_tiles(pieces)], 1)
                part = dot_nn(probs, own_value)
                mixed[block] = part if which == 0 else mixed[block] + part
        target = pl.ds(pl.multiple_of(owner * cols + offset, width), width)
        for block in range(count // TILE):
            rows = slice(block * TILE, (block + 1) * TILE)
            mix_ref[rows, target] = mixed[block].astype(BF16)
        return carry

    lax.fori_loop(0, cols // width, pair, 0)


def front_body(
    size, groups, head_size, span_ref, routes_ref, gain_ref, table_ref, ones_ref, router_ref, tok_hbm,
    cot_hbm,
    qkv_shard, out_shard, in_shard,
    col_ref, gate_ref, sent_gate_ref, qkvw_out, outw_out, qkv_out, mixed_out, hidden_out, norm_out,
    sent_out, outer_out, gate_out,
    tok, cot, qkvw, outw, qkv, mixed, hidden, norm, sent, outer, mask, row, diag_ref, load_sems, save_sems,
    shard_sems, outer_send, outer_got,
):
    me, place = lax.axis_index("dp"), lax.axis_index("wshard")
    near, far = flip(place, 1, groups), flip(place, 2, groups)
    peers = [("dp", flip(me, step, size)) for step in range(1, size)]
    greet(peers + [("wshard", near), ("wshard", far)])

    sources = (qkv_shard, out_shard, in_shard.at[0, : gate_out.shape[1]])

    def held(item, group):
        if item == 0:
            return qkvw.at[group]
        if item == 1:
            return outw.at[group]
        return gate_out.at[group - 2]

    def shard_copy(kind, item):
        source = held(item, 2) if kind == 2 else sources[item]
        return remote_copy(
            source, held(item, (1, 2, 3)[kind]), shard_sems.at[kind, item, 0],
            shard_sems.at[kind, item, 1], "wshard", far if kind == 1 else near,
        )

    shard_copy(1, 0).start()
    for item in range(2):
        shard_copy(0, item).start()
    loads = [
        pltpu.make_async_copy(source, target, load_sems.at[i])
        for i, (source, target) in enumerate(
            ((cot_hbm, cot), (tok_hbm, tok), (qkv_shard, qkvw.at[0]), (out_shard, outw.at[0]))
        )
    ]
    for copy in loads:
        copy.start()

    experts, capacity = size, sent.shape[1]
    count = tok.shape[0]
    slots = route_slots(experts, capacity, routes_ref[...])
    row[...] = slots
    col_ref[...] = slots.astype(F32).T.astype(I32)
    loads[0].wait()

    def place_outer(expert, carry):
        outer[expert] = dot_nn(onehot_rows(expert * capacity, capacity, row[...]), cot[...]).astype(BF16)
        return carry

    lax.fori_loop(0, experts, place_outer, 0)
    fill_mask(mask, span_ref[0])
    diag_ref[...] = spread_bias(table_ref, ones_ref)
    loads[1].wait()
    unit, _ = unit_norm(tok[...].astype(F32))
    norm[...] = (unit * gain_ref[0:1, :]).astype(BF16)
    loads[2].wait()

    def outer_copy(source, target, peer):
        return remote_copy(
            outer.at[source], outer_out.at[target], outer_send.at[source], outer_got.at[target],
            "dp", peer,
        )

    own_outer = pltpu.make_async_copy(outer.at[me], outer_out.at[me], load_sems.at[4])
    own_outer.start()
    turns = turns_of(size)

    def send_outer(turn):
        for step in turns[turn]:
            peer = flip(me, step, size)
            outer_copy(peer, me, peer).start()

    send_outer(0)

    def one_group(group, carry):
        @pl.when(group == 1)
        def _():
            send_outer(1)
            shard_copy(0, 0).wait_recv()

        @pl.when(group == 2)
        def _():
            shard_copy(1, 0).wait()
            shard_copy(2, 0).start()
            shard_copy(1, 1).start()

        @pl.when(group == 3)
        def _():
            send_outer(2)
            shard_copy(2, 0).wait_recv()

        project_and_attend(
            place, group, groups, head_size, norm, diag_ref, qkvw, qkv, mixed, mask
        )
        return carry

    lax.fori_loop(0, groups, one_group, 0)
    saves = [
        pltpu.make_async_copy(source, target, save_sems.at[i])
        for i, (source, target) in enumerate(
            (
                (qkvw, qkvw_out), (qkv, qkv_out), (mixed, mixed_out), (outw, outw_out),
                (hidden, hidden_out), (norm, norm_out), (sent, sent_out),
            )
        )
    ]
    for copy in saves[:3]:
        copy.start()
    loads[3].wait()
    shard_copy(0, 1).wait_recv()
    shard_copy(1, 1).wait()
    shard_copy(2, 1).start()
    shard_copy(1, 2).start()

    shard_copy(2, 1).wait_recv()
    saves[3].start()
    for group in range(groups):
        cols = outw.shape[2]
        lanes = pl.ds(pl.multiple_of(flip(place, group, groups) * cols, cols), cols)
        hidden[:, lanes] = tok[:, lanes].astype(F32) + dot_nn(mixed[...], outw[group])
    saves[4].start()
    unit, _ = unit_norm(hidden[...])
    norm[...] = (unit * gain_ref[1:2, :]).astype(BF16)
    saves[5].start()

    def place_sent(expert, carry):
        sent[expert] = dot_nn(onehot_rows(expert * capacity, capacity, row[...]), norm[...]).astype(BF16)
        return carry

    lax.fori_loop(0, experts, place_sent, 0)
    saves[6].start()
    logits = dot_nt(norm[...], router_ref[...])
    slots = [col_ref[:, k : k + 1] for k in range(2)]
    lane = iota(logits.shape, 1)
    chosen = []
    for k in range(2):
        own = (lane * capacity <= slots[k]) & (slots[k] < (lane + 1) * capacity)
        chosen.append(jnp.sum(jnp.where(own, logits, 0.0), -1, keepdims=True))
    top = jnp.maximum(chosen[0], chosen[1])
    powers = [jnp.exp(c - top) for c in chosen]
    gates = [power / (powers[0] + powers[1]) for power in powers]
    for k in range(2):
        gate_ref[:, k : k + 1] = gates[k]
    lane = iota((count, sent_gate_ref.shape[2]), 1)
    for expert in range(experts):
        label = jnp.where(lane < capacity, lane + expert * capacity, -1)
        part = 0.0
        for k in range(2):
            part = part + jnp.where(label == slots[k], gates[k], 0.0)
        line = jnp.sum(part, 0, keepdims=True)
        sent_gate_ref[expert] = jnp.broadcast_to(line, sent_gate_ref.shape[1:])

    shard_copy(1, 2).wait()
    shard_copy(2, 2).start()
    own_outer.wait()
    for copy in saves:
        copy.wait()
    for _, peer in peers:
        outer_copy(peer, me, peer).wait_send()
        outer_copy(me, peer, peer).wait_recv()
    for item in range(2):
        shard_copy(0, item).wait_send()
        shard_copy(2, item).wait_send()
    shard_copy(2, 2).wait()


def front(
    span, routes, gains, table_t, ones, router_t, tokens, cotangent, shards, head_size, capacity
):
    count, width = tokens.shape
    size, groups = lax.axis_size("dp"), lax.axis_size("wshard")
    qkv_shard, out_shard, in_shard = shards
    cols = out_shard.shape[1]
    lanes = -(-capacity // TILE) * TILE
    dma = pltpu.SemaphoreType.DMA
    block = (size, capacity, width)
    return pl.pallas_call(
        functools.partial(front_body, size, groups, head_size),
        out_shape=(
            shape_of((count, 8), I32),
            shape_of((count, 2), F32),
            shape_of((size, EXTRA, lanes), F32),
            shape_of((groups, *qkv_shard.shape), BF16),
            shape_of((groups, *out_shard.shape), BF16),
            shape_of((groups, 3, count, cols), BF16),
            shape_of((count, width), BF16),
            shape_of((count, width), F32),
            shape_of((count, width), BF16),
            shape_of(block, BF16),
            shape_of(block, BF16),
            shape_of((2, in_shard.shape[1] // 32 * 16, width), BF16),
        ),
        in_specs=[SMEM] + [VMEM] * 5 + [ANY] * 5,
        out_specs=(VMEM,) * 3 + (ANY,) * 9,
        scratch_shapes=[
            pltpu.VMEM((count, width), BF16),
            pltpu.VMEM((count, width), BF16),
            pltpu.VMEM((groups, *qkv_shard.shape), BF16),
            pltpu.VMEM((groups, *out_shard.shape), BF16),
            pltpu.VMEM((groups, 3, count, cols), BF16),
            pltpu.VMEM((count, width), BF16),
            pltpu.VMEM((count, width), F32),
            pltpu.VMEM((count, width), BF16),
            pltpu.VMEM(block, BF16),
            pltpu.VMEM(block, BF16),
            pltpu.VMEM((count, count), F32),
            pltpu.VMEM((8, count), I32),
            pltpu.VMEM((table_t.shape[0], ones.shape[1]), F32),
            dma((5,)),
            dma((7,)),
            dma((3, 3, 2)),
            dma((size,)),
            dma((size,)),
        ],
        cost_estimate=pl.CostEstimate(flops=LIGHT, bytes_accessed=LIGHT, transcendentals=0),
        compiler_params=pltpu.CompilerParams(
            collective_id=1, has_side_effects=True, vmem_limit_bytes=60_000_000
        ),
        name="front",
    )(span, routes.T, gains, table_t, ones, router_t, tokens, cotangent, *shards)


def flip(value, change, size):
    result = 0
    bit = 1
    while bit < size:
        one, two = lax.rem(lax.div(value, bit), 2), lax.rem(lax.div(change, bit), 2)
        result = result + bit * (one + two - 2 * one * two)
        bit *= 2
    return result


def column_of(row, size):
    spot = iota((size, row.shape[1]), 0) == iota((size, row.shape[1]), 1)
    return jnp.sum(jnp.where(spot, row, 0.0), 1, keepdims=True)


def row_of(column, lanes):
    spot = iota((column.shape[0], lanes), 0) == iota((column.shape[0], lanes), 1)
    return jnp.sum(jnp.where(spot, column, 0.0), 0, keepdims=True)


def moe_body(
    size, groups, chunk, sent_ref, gates_ref, outer_ref, own_in, own_down, far_gate, *refs
):
    back_out, extra_out, made_out, grad_out, moved_out = refs[:5]
    (
        buf, rows, gates, outer, low_outer, made_sum, back_sum, act, low, stage, extra_stage,
        made, grad_stage, weight_sems, shard_sems, send_sems, recv_sems, give_sems, take_sems, own_sems,
        save_sems, grad_sems, moved_sem, sum_sems,
    ) = refs[5:]
    share = own_down.shape[0]
    part_size = share * groups // 2
    capacity, width = outer.shape[1:]
    both = 2 * capacity
    me = lax.axis_index("dp")
    pairs = size // 2
    my_pair = lax.div(me, 2)
    mesh_id = pl.DeviceIdType.MESH

    place = lax.axis_index("wshard")
    near, far = flip(place, 1, groups), flip(place, 2, groups)
    peers = [("dp", flip(me, step, size)) for step in range(1, size)]
    greet(peers + [("wshard", near), ("wshard", far)])

    def remote(source, target, sent, got, peer):
        return pltpu.make_async_remote_copy(
            src_ref=source, dst_ref=target, send_sem=sent, recv_sem=got,
            device_id={"dp": peer}, device_id_type=mesh_id,
        )

    def forth(source, target, peer):
        return (
            remote(sent_ref.at[source], rows.at[target], send_sems.at[source, 0],
                   recv_sems.at[target, 0], peer),
            remote(gates_ref.at[source], gates.at[target], send_sems.at[source, 1],
                   recv_sems.at[target, 1], peer),
        )

    def back_copies(source, target, peer):
        return (
            remote(stage.at[source], back_out.at[target], give_sems.at[source, 0],
                   take_sems.at[target, 0], peer),
            remote(extra_stage.at[source], extra_out.at[target], give_sems.at[source, 1],
                   take_sems.at[target, 1], peer),
        )

    own = (
        pltpu.make_async_copy(sent_ref.at[me], rows.at[me], own_sems.at[0]),
        pltpu.make_async_copy(gates_ref.at[me], gates.at[me], own_sems.at[1]),
        pltpu.make_async_copy(outer_ref, outer, own_sems.at[2]),
    )
    own_back = (
        pltpu.make_async_copy(stage.at[me], back_out.at[me], own_sems.at[3]),
        pltpu.make_async_copy(extra_stage.at[me], extra_out.at[me], own_sems.at[4]),
    )
    for copy in own:
        copy.start()
    turns = turns_of(size)

    def send_rows(steps):
        for step in steps:
            peer = flip(me, step, size)
            for copy in forth(peer, me, peer):
                copy.start()

    send_rows(turns[2])
    send_rows(turns[0])

    begun = far_gate.shape[1]

    def home(c, group, first, count):
        return buf.at[c, pl.ds(group * share + first, count)]

    loads = [
        pltpu.make_async_copy(own_in, buf.at[0:2, pl.ds(0, share)], weight_sems.at[0]),
        pltpu.make_async_copy(own_down, home(2, 0, 0, share), weight_sems.at[1]),
    ]
    loads += [
        pltpu.make_async_copy(far_gate.at[i], home(0, 2 + i, 0, begun), weight_sems.at[2 + i])
        for i in range(2)
    ]
    near_copies = [
        remote_copy(own_in, buf.at[0:2, pl.ds(share, share)], shard_sems.at[0, 0, 0],
                    shard_sems.at[0, 0, 1], "wshard", near),
        remote_copy(own_down, home(2, 1, 0, share), shard_sems.at[0, 1, 0],
                    shard_sems.at[0, 1, 1], "wshard", near),
    ]
    rest = ((0, begun, share - begun), (1, 0, share), (2, 0, share))

    def far_copy(c):
        _, first, count = rest[c]
        source = own_down if c == 2 else own_in.at[c]
        return remote_copy(source.at[pl.ds(first, count)], home(c, 2, first, count),
                           shard_sems.at[1, c, 0], shard_sems.at[1, c, 1], "wshard", far)

    def onward_copy(c):
        _, first, count = rest[c]
        return remote_copy(home(c, 2, first, count), home(c, 3, first, count),
                           shard_sems.at[2, c, 0], shard_sems.at[2, c, 1], "wshard", near)

    far_copy(0).start()
    far_copy(1).start()
    for copy in loads + near_copies:
        copy.start()
    for copy in own:
        copy.wait()

    def hidden_part(pair, base):
        spot = pl.ds(pl.multiple_of(pair * both, both), both)
        two = pl.ds(2 * pair, 2)
        these = rows[two].reshape(both, width)
        outers = low_outer[spot, :]
        for first in range(0, part_size, chunk):
            last = min(first + chunk, part_size)
            part, lanes = slice(base + first, base + last), slice(first, last)
            gate, up = dot_nt(these, buf[0, part, :]), dot_nt(these, buf[1, part, :])
            act_grad = dot_nt(outers, buf[2, part, :])
            square = gate * gate
            inner = gate * (0.7978845608028654 + (0.7978845608028654 * 0.044715) * square)
            rise = 0.5 + 0.5 * jnp.tanh(inner)
            bent = gate * rise
            act[spot, lanes] = (bent * up).astype(BF16)
            slope = rise + bent * (1.0 - rise) * (
                2 * 0.7978845608028654 + (6 * 0.7978845608028654 * 0.044715) * square
            )
            low[0, spot, lanes] = (act_grad * up * slope).astype(BF16)
            low[1, spot, lanes] = (act_grad * bent).astype(BF16)
        whole = slice(base, base + part_size)
        result = dot_nn(act[spot, :], buf[2, whole, :])
        back = dot_nn(low[0, spot, :], buf[0, whole, :]) + dot_nn(low[1, spot, :], buf[1, whole, :])
        return spot, result, back

    def near_step(step, carry):
        pair = flip(my_pair, step, pairs)
        first = 2 * pair

        @pl.when(step == 1)
        def _():
            send_rows(turns[1])

        @pl.when(step == pairs // 2)
        def _():
            for c in range(2):
                far_copy(c).wait()
                onward_copy(c).start()
            far_copy(2).start()

        @pl.when(step == 0)
        def _():
            peer = flip(me, 1, size)
            for copy in forth(me, peer, peer):
                copy.wait_recv()

        @pl.when(step > 0)
        def _():
            for which in range(2):
                for copy in forth(me, first + which, first + which):
                    copy.wait_recv()

        for which in range(2):
            gate = column_of(gates[first + which, 0:1, :], capacity)
            spot = pl.ds(pl.multiple_of((first + which) * capacity, capacity), capacity)
            low_outer[spot, :] = (outer[first + which].astype(F32) * gate).astype(BF16)
        spot, result, back = hidden_part(pair, 0)
        made_sum[spot, :] = result
        back_sum[spot, :] = back
        return carry

    def sent_all(copies):
        for remote_one, copy in copies:
            if remote_one:
                copy.wait_send()
            else:
                copy.wait()

    def weight_grads(half):
        every = rows[...].reshape(size * capacity, width)
        outers = low_outer[...]
        count = 0
        base = half * part_size
        waiting = {}
        for c in range(3):
            left = act if c == 2 else low.at[c]
            for first in range(0, part_size, 2 * chunk):
                last = min(first + 2 * chunk, part_size)
                slot = count % 2
                sent_all(waiting.pop(slot, ()))
                piece = dot_tn(left[:, first:last], outers if c == 2 else every)
                grad_stage[slot, : last - first, :] = piece.astype(BF16)
                copies = []
                begin = base + first
                while begin < base + last:
                    group = begin // share
                    end = min(base + last, (group + 1) * share)
                    source = grad_stage.at[slot, pl.ds(begin - base - first, end - begin)]
                    spot = pl.ds(begin - group * share, end - begin)
                    sem = grad_sems.at[slot, len(copies)]
                    if group % 2:
                        target = moved_out.at[group // 2, c, spot]
                        copies.append((True, remote_copy(source, target, sem, moved_sem, "wshard", near)))
                    else:
                        target = grad_out.at[group // 2, c, spot]
                        copies.append((False, pltpu.make_async_copy(source, target, sem)))
                    begin = end
                for _, copy in copies:
                    copy.start()
                waiting[slot] = copies
                count += 1
        for copies in waiting.values():
            sent_all(copies)

    for copy in loads[:2]:
        copy.wait()
    for copy in near_copies:
        copy.wait_recv()
    lax.fori_loop(0, pairs, near_step, 0)
    weight_grads(0)

    def far_step(step, carry):
        pair = flip(my_pair, pairs - 1 - step, pairs)
        first = 2 * pair
        spot, result, back = hidden_part(pair, part_size)
        result = (made_sum[spot, :] + result).astype(BF16)
        back = (back_sum[spot, :] + back).astype(BF16)
        two = pl.ds(first, 2)
        made[two] = result.reshape(2, capacity, width)
        stage[two] = back.reshape(2, capacity, width)
        for which in range(2):
            grads = outer[first + which].astype(F32) * made[first + which].astype(F32)
            line = row_of(jnp.sum(grads, -1, keepdims=True), extra_stage.shape[2])
            extra_stage[first + which] = jnp.broadcast_to(line, extra_stage.shape[1:])
        pltpu.make_async_copy(made.at[two], made_out.at[two], save_sems.at[step]).start()

        @pl.when(step < pairs - 1)
        def _():
            for which in range(2):
                for copy in back_copies(first + which, me, first + which):
                    copy.start()

        @pl.when(step == pairs - 1)
        def _():
            peer = flip(me, 1, size)
            for copy in back_copies(peer, me, peer):
                copy.start()
            for copy in own_back:
                copy.start()

        return carry

    far_copy(2).wait()
    onward_copy(2).start()
    for copy in loads[2:]:
        copy.wait()
    for c in range(3):
        onward_copy(c).wait_recv()
    lax.fori_loop(0, pairs, far_step, 0)
    weight_grads(1)
    remote_copy(moved_out, moved_out, moved_sem, moved_sem, "wshard", near).wait_recv()

    corner = (pl.ds(0, share), pl.ds(0, width))
    rooms = ((low.at[0], act), (low.at[1], low_outer))
    pieces = [(g, c) for g in (1, 0) for c in range(3)]

    def fetch(i):
        slot = i % 2
        return [
            pltpu.make_async_copy(source.at[pieces[i]], room.at[corner], sum_sems.at[slot, k])
            for k, (source, room) in enumerate(zip((grad_out, moved_out), rooms[slot]))
        ]

    def put(i):
        slot = i % 2
        return pltpu.make_async_copy(
            rooms[slot][0].at[corner], grad_out.at[pieces[i]], sum_sems.at[slot, 2]
        )

    for i in range(2):
        for copy in fetch(i):
            copy.start()
    for i in range(len(pieces)):
        for copy in fetch(i):
            copy.wait()
        one, other = rooms[i % 2]

        def add_rows(block, carry):
            spot = (pl.ds(pl.multiple_of(block * 64, 64), 64), slice(0, width))
            one[spot] = (one[spot].astype(F32) + other[spot].astype(F32)).astype(BF16)
            return carry

        lax.fori_loop(0, share // 64, add_rows, 0)
        put(i).start()
        if i + 2 < len(pieces):
            put(i).wait()
            for copy in fetch(i + 2):
                copy.start()
    for i in range(len(pieces) - 2, len(pieces)):
        put(i).wait()
    for copy in own_back:
        copy.wait()
    for copy in near_copies:
        copy.wait_send()
    for c in range(3):
        onward_copy(c).wait_send()
    for step in range(pairs):
        two = pl.ds(2 * flip(my_pair, pairs - 1 - step, pairs), 2)
        pltpu.make_async_copy(made.at[two], made_out.at[two], save_sems.at[step]).wait()
    for step in range(1, size):
        peer = flip(me, step, size)
        for copy in forth(peer, me, peer):
            copy.wait_send()
        for copy in back_copies(peer, me, peer):
            copy.wait_send()
        for copy in back_copies(me, peer, peer):
            copy.wait_recv()


def moe(sent, gates, outer, own_in, own_down, far_gate, chunk=256):
    size, capacity, width = sent.shape
    groups = lax.axis_size("wshard")
    share = own_down.shape[0]
    part = share * groups // 2
    total = size * capacity
    extra = gates.shape[1:]
    dma = pltpu.SemaphoreType.DMA
    result = pl.pallas_call(
        functools.partial(moe_body, size, groups, chunk),
        out_shape=(
            shape_of((size, capacity, width), BF16),
            shape_of((size, *extra), F32),
            shape_of((size, capacity, width), BF16),
        )
        + (shape_of((2, 3, share, width), BF16),) * 2,
        in_specs=[ANY] * 6,
        out_specs=(ANY,) * 5,
        scratch_shapes=[
            pltpu.VMEM((3, share * groups, width), BF16),
            pltpu.VMEM((size, capacity, width), BF16),
            pltpu.VMEM((size, *extra), F32),
            pltpu.VMEM((size, capacity, width), BF16),
            pltpu.VMEM((total, width), BF16),
            pltpu.VMEM((total, width), F32),
            pltpu.VMEM((total, width), F32),
            pltpu.VMEM((total, part), BF16),
            pltpu.VMEM((2, total, part), BF16),
            pltpu.VMEM((size, capacity, width), BF16),
            pltpu.VMEM((size, *extra), F32),
            pltpu.VMEM((size, capacity, width), BF16),
            pltpu.VMEM((2, 2 * chunk, width), BF16),
            dma((4,)),
            dma((3, 3, 2)),
            dma((size, 2)),
            dma((size, 2)),
            dma((size, 2)),
            dma((size, 2)),
            dma((5,)),
            dma((size // 2,)),
            dma((2, 3)),
            dma,
            dma((2, 3)),
        ],
        cost_estimate=pl.CostEstimate(flops=LIGHT, bytes_accessed=LIGHT, transcendentals=0),
        compiler_params=pltpu.CompilerParams(
            collective_id=0, has_side_effects=True, vmem_limit_bytes=66_000_000
        ),
        name="experts",
    )(sent, gates, outer, own_in, own_down, far_gate)
    return result[:4]


def expert_body(groups, chunk, rows_ref, outer_ref, gate_ref, *refs):
    in_refs, down_refs = refs[:groups], refs[groups : 2 * groups]
    made_ref, back_ref, outer_out_ref, gate_grad_ref = refs[2 * groups : 2 * groups + 4]
    act_ref, low_ref, buf_ref, sems = refs[2 * groups + 4 :]
    share = down_refs[0].shape[0]
    hidden = share * groups

    def copies(group):
        spot = pl.ds(group * share, share)
        return (
            pltpu.make_async_copy(in_refs[group], buf_ref.at[0:2, spot], sems.at[2 * group]),
            pltpu.make_async_copy(down_refs[group], buf_ref.at[2, spot], sems.at[2 * group + 1]),
        )

    @pl.when(pl.program_id(0) == 0)
    def _():
        for group in range(groups):
            for copy in copies(group):
                copy.start()

    rows = rows_ref[...]
    low_outer = (outer_ref[...].astype(F32) * gate_ref[...]).astype(BF16)
    outer_out_ref[...] = low_outer

    @pl.when(pl.program_id(0) == 0)
    def _():
        for group in range(groups):
            for copy in copies(group):
                copy.wait()

    for first in range(0, hidden, chunk):
        part = slice(first, first + chunk)
        gate, up = dot_nt(rows, buf_ref[0, part, :]), dot_nt(rows, buf_ref[1, part, :])
        act_grad = dot_nt(low_outer, buf_ref[2, part, :])
        square = gate * gate
        inner = gate * (0.7978845608028654 + (0.7978845608028654 * 0.044715) * square)
        rise = 0.5 + 0.5 * jnp.tanh(inner)
        bent = gate * rise
        act_ref[:, part] = (bent * up).astype(BF16)
        slope = rise + bent * (1.0 - rise) * (
            2 * 0.7978845608028654 + (6 * 0.7978845608028654 * 0.044715) * square
        )
        low_ref[0, :, part] = (act_grad * up * slope).astype(BF16)
        low_ref[1, :, part] = (act_grad * bent).astype(BF16)
    made = dot_nn(act_ref[...], buf_ref[2]).astype(BF16)
    made_ref[...] = made
    back = dot_nn(low_ref[0], buf_ref[0]) + dot_nn(low_ref[1], buf_ref[1])
    back_ref[...] = back.astype(BF16)
    gate_grad_ref[...] = jnp.sum(
        outer_ref[...].astype(F32) * made.astype(F32), -1, keepdims=True
    )


def experts_pass(rows, outer, gate_column, in_weights, down_weights, block=320, chunk=256):
    total, width = rows.shape
    groups = len(in_weights)
    hidden = down_weights[0].shape[0] * groups
    row_spec = pl.BlockSpec((block, width), lambda i: (i, 0))
    column = pl.BlockSpec((block, 1), lambda i: (i, 0))
    wide = pl.BlockSpec((block, hidden), lambda i: (i, 0))
    both = pl.BlockSpec((2, block, hidden), lambda i: (0, i, 0))
    return pl.pallas_call(
        functools.partial(expert_body, groups, chunk),
        grid=(total // block,),
        out_shape=(
            shape_of((total, width), BF16),
            shape_of((total, width), BF16),
            shape_of((total, width), BF16),
            shape_of((total, 1), F32),
            shape_of((total, hidden), BF16),
            shape_of((2, total, hidden), BF16),
        ),
        in_specs=[row_spec, row_spec, column] + [ANY] * (2 * groups),
        out_specs=(row_spec, row_spec, row_spec, column, wide, both),
        scratch_shapes=[
            pltpu.VMEM((3, hidden, width), BF16),
            pltpu.SemaphoreType.DMA((2 * groups,)),
        ],
        cost_estimate=pl.CostEstimate(flops=LIGHT, bytes_accessed=LIGHT, transcendentals=0),
        name="experts",
    )(rows, outer, gate_column, *in_weights, *down_weights)


def moe_plain(sent, gates, outer, own_in, own_down, far_gate):
    in_weights, down_weights = [own_in], [own_down]
    for bit in (1, 2):
        in_weights += [swap(w, "wshard", bit) for w in in_weights]
        down_weights += [swap(w, "wshard", bit) for w in down_weights]
    size, capacity, width = sent.shape
    total = size * capacity
    rows = exchange(sent.reshape(total, width), "dp").reshape(total, width)
    gate_column = lax.all_to_all(gates, "dp", 0, 0, tiled=True)[:, 0, :capacity].reshape(total, 1)
    made, back, outer_low, gate_grads, act, low = experts_pass(
        rows, outer.reshape(total, width), gate_column, in_weights, down_weights
    )
    extra = jnp.pad(gate_grads.reshape(size, 1, capacity), ((0, 0), (0, EXTRA - 1), (0, 0)))
    extra = lax.all_to_all(extra, "dp", 0, 0, tiled=True)
    share = down_weights[0].shape[0]
    grads = []
    for group in range(len(in_weights)):
        part = slice(group * share, (group + 1) * share)
        pieces = [dot_tn(low[c, :, part], rows) for c in range(2)]
        grads.append(jnp.stack(pieces + [dot_tn(act[:, part], outer_low)]).astype(BF16))
    shape = (size, capacity, width)
    moved = jnp.stack([swap(grads[g], "wshard", 1) for g in (1, 3)])
    sums = (jnp.stack(grads[::2]).astype(F32) + moved.astype(F32)).astype(BF16)
    return exchange(back, "dp"), extra, made.reshape(shape), sums


def rear_body(
    size, groups, head_size, remote_made, span_ref, gain_ref, table_ref, ones_ref, router_ref, col_ref, gate_ref,
    extra_ref, tok_hbm, cot_hbm, hidden_hbm, norm_hbm, mixed_hbm, rows_hbm, made_hbm, outw_hbm,
    qkvw_hbm, qkv_hbm, far_hbm,
    output_ref, grad_ref, gains_out, table_out, router_out, sum_out, sum_out_two, far_out,
    tok, cot, hidden, norm, mixed, rows, made, outw, qkvw, qkv, norm_t, mask, grad_hidden,
    grads, probs_ref, scores_ref, diag_sums, wo, wo_got, wg, wg_got, total,
    total_got, sum_ref, early_ref, early_got, late_ref, late_got, diag_ref,
    load_sems, weight_sems, made_send, made_got, part_sems, total_sems, small_sems, far_sems,
):
    me, place = lax.axis_index("dp"), lax.axis_index("wshard")
    near, far = flip(place, 1, groups), flip(place, 2, groups)
    dp_bits, shard_bits = bits_below(size), bits_below(groups)
    peers = [("dp", flip(me, step, size)) for step in range(1, size)]
    greet(peers + [("wshard", near), ("wshard", far)])
    count, width = tok.shape
    blocks = count // TILE
    experts = size
    capacity = rows.shape[0] // experts
    cols = outw.shape[2]
    two_heads = 2 * head_size
    branch, mixgrad, norm_grad = cot, norm, hidden

    loads = [
        pltpu.make_async_copy(source, target, load_sems.at[i])
        for i, (source, target) in enumerate(
            (
                (rows_hbm, rows), (norm_hbm, norm), (hidden_hbm, hidden), (cot_hbm, cot),
                (mixed_hbm, mixed), (outw_hbm, outw), (tok_hbm, tok), (qkv_hbm, qkv),
                (made_hbm.at[me], made.at[me]) if remote_made else (made_hbm, rows),
            )
        )
    ]
    for copy in loads[: 9 if remote_made else 8]:
        copy.start()

    def far_copy(piece):
        return remote_copy(
            far_hbm.at[1, piece], far_out.at[piece], far_sems.at[piece, 0], far_sems.at[piece, 1],
            "wshard", far,
        )

    far_copy(0).start()

    def weight_load(step):
        slot = lax.rem(step, 2)
        return pltpu.make_async_copy(
            qkvw_hbm.at[groups - 1 - step], qkvw.at[slot], weight_sems.at[slot]
        )

    hidden_again = pltpu.make_async_copy(hidden_hbm, hidden, load_sems.at[9])

    def made_copy(source, target, peer):
        return remote_copy(
            made_hbm.at[source], made.at[target], made_send.at[source], made_got.at[target], "dp",
            peer,
        )

    turns = turns_of(size)

    def send_made(turn):
        if remote_made:
            for step in turns[turn]:
                peer = flip(me, step, size)
                made_copy(peer, me, peer).start()

    send_made(0)

    exchanges = [("wshard", place, bit, groups) for bit in shard_bits]
    exchanges += [("dp", me, bit, size) for bit in dp_bits]

    def small_copy(kind, ref, got, step):
        axis, index, bit, length = exchanges[step]
        return remote_copy(
            ref, got.at[step], small_sems.at[kind, step, 0], small_sems.at[kind, step, 1], axis,
            flip(index, bit, length),
        )

    def small_step(kind, ref, got, step):
        now, before = step % 2, (step + 1) % 2
        if step > 0:
            small_copy(kind, ref.at[before], got, step - 1).wait()
            ref[now] = ref[before] + got[step - 1]
        if step < len(exchanges):
            small_copy(kind, ref.at[now], got, step).start()

    slots = [col_ref[:, k : k + 1] for k in range(2)]
    gates = [gate_ref[:, k : k + 1] for k in range(2)]
    lane = iota((count, extra_ref.shape[2]), 1)
    picked = [0.0, 0.0]
    for copy in loads[:1]:
        copy.wait()
    grads_in = 0.0
    for expert in range(experts):
        label = jnp.where(lane < capacity, lane + expert * capacity, -1)
        for k in range(2):
            picked[k] = picked[k] + jnp.where(label == slots[k], extra_ref[expert, 0:1, :], 0.0)
    gate_grads = [jnp.sum(p, -1, keepdims=True) for p in picked]
    mean = gates[0] * gate_grads[0] + gates[1] * gate_grads[1]
    lane = iota((count, 3 * experts), 1)
    part = (lane >= experts).astype(I32) + (lane >= 2 * experts).astype(I32)
    label = lane - part * experts
    logit_grads = 0.0
    for k in range(2):
        own = (label * capacity <= slots[k]) & (slots[k] < (label + 1) * capacity)
        logit_grads = logit_grads + jnp.where(own, gates[k] * (gate_grads[k] - mean), 0.0)
    high, middle, low = split_three(logit_grads)
    split = jnp.where(part == 0, high, jnp.where(part == 1, middle, low)).astype(BF16)
    hits = [onehot_columns(slots[k], 0, experts * capacity) for k in range(2)]
    hits = (hits[0] | hits[1]).astype(F32).astype(BF16)
    for copy in loads[1:4]:
        copy.wait()
    normed_grad = dot_nn(hits, rows[...])
    normed_grad = normed_grad + dot_nn(split, router_ref[...])
    router_grad = dot_tn(split, norm[...])
    early_ref[0, :experts, :] = (
        router_grad[:experts] + router_grad[experts : 2 * experts] + router_grad[2 * experts :]
    )
    unit, recip = unit_norm(hidden[...])
    early_ref[0, experts:, :] = jnp.broadcast_to(
        jnp.sum(normed_grad * unit, 0, keepdims=True), (EXTRA, width)
    )
    small_step(0, early_ref, early_got, 0)
    scaled = normed_grad * gain_ref[1:2, :]
    back = recip * (scaled - unit * jnp.mean(scaled * unit, -1, keepdims=True))
    grad_hidden[...] = cot[...].astype(F32) + back
    branch[...] = grad_hidden[...].astype(BF16)
    for copy in loads[4:6]:
        copy.wait()
    mixed_t = mixed[...].T
    result = 0.0

    def part_copy(item, source, target, kind, axis, peer):
        return remote_copy(
            source, target, part_sems.at[item, kind, 0], part_sems.at[item, kind, 1], axis, peer
        )

    def out_copy(kind):
        return part_copy(
            0, wo.at[(3, 1, 2)[kind]], wo_got.at[kind], kind, "wshard", far if kind == 2 else near
        )

    def qkv_copy(kind):
        return part_copy(
            1, wg.at[(2, 0, 1)[kind]], wg_got.at[kind], kind, "wshard", far if kind == 2 else near
        )

    for group in reversed(range(groups)):
        lanes = pl.ds(pl.multiple_of(flip(place, group, groups) * cols, cols), cols)
        piece = branch[:, lanes]
        result = result + dot_nt(piece, outw[group])
        wo[group] = dot_nn(mixed_t, piece).astype(BF16)
        if group == 3:
            out_copy(0).start()
        if group == 1:
            out_copy(1).start()
    mixgrad[...] = result.astype(BF16)
    for copy in loads[6:8]:
        copy.wait()
    weight_load(0).start()
    unit, _ = unit_norm(tok[...].astype(F32))
    norm_t[...] = (unit * gain_ref[0:1, :]).astype(BF16).T
    fill_mask(mask, span_ref[0])
    diag_ref[...] = spread_bias(table_ref, ones_ref)
    norm_grad[...] = jnp.zeros_like(norm_grad)

    def attend_group(step):
        group = groups - 1 - step
        slot = lax.rem(step, 2)
        weight_load(step).wait()

        @pl.when(step < groups - 1)
        def _():
            weight_load(step + 1).start()

        owner = flip(place, group, groups)
        heads = cols // head_size

        def pair(p, carry):
            offset = pl.multiple_of(p * two_heads, two_heads)
            lanes = pl.ds(offset, two_heads)
            query, keys, value = (qkv[group, c, :, lanes] for c in range(3))
            outer = mixgrad[:, pl.ds(pl.multiple_of(owner * cols + offset, two_heads), two_heads)]
            query_sum, key_sum, value_sum = [None] * blocks, None, None
            for which in range(2):
                head = owner * heads + 2 * p + which
                own = head_lanes(which, head_size)
                own_query, own_key, own_outer = query * own, keys * own, outer * own
                shrunk = own_query * 0.125
                tiles, far_bias = bias_tiles(diag_ref[pl.ds(head, 1), :])
                near_sums, far_sums = [None] * 3, [None] * 2
                for block in range(blocks):
                    piece = slice(block * TILE, (block + 1) * TILE)
                    probs = softmax_tiles(
                        score_tiles(block, shrunk[piece], keys, tiles, far_bias, mask)
                    )
                    prob_grads = dot_nt(own_outer[piece], value)
                    prob_grads = [prob_grads[:, j * TILE : (j + 1) * TILE] for j in range(blocks)]
                    delta = functools.reduce(jnp.add, [a * b for a, b in zip(probs, prob_grads)])
                    delta = jnp.sum(delta, -1, keepdims=True)
                    lows = [(a * (b - delta)).astype(BF16) for a, b in zip(probs, prob_grads)]
                    for other in range(blocks):
                        step = block - other
                        wide = lows[other].astype(F32)
                        if abs(step) >= 2:
                            side = 0 if step > 0 else 1
                            old = far_sums[side]
                            far_sums[side] = wide if old is None else old + wide
                        else:
                            old = near_sums[step + 1]
                            near_sums[step + 1] = wide if old is None else old + wide
                    probs_ref[which, piece, :] = jnp.concatenate([t.astype(BF16) for t in probs], 1)
                    lows = jnp.concatenate(lows, 1)
                    scores_ref[which, piece, :] = lows
                    more = dot_nn(lows, own_key)
                    query_sum[block] = more if which == 0 else query_sum[block] + more
                more = dot_tn(scores_ref[which], own_query)
                key_sum = more if which == 0 else key_sum + more
                more = dot_tn(probs_ref[which], own_outer)
                value_sum = more if which == 0 else value_sum + more
                for step in range(3):
                    wide = jnp.concatenate([near_sums[step], jnp.zeros((TILE, TILE), F32)], 1)
                    half = TILE // 2
                    while half:
                        turned = pltpu.roll(wide[half:], 2 * TILE - half, 1)
                        wide = wide[:half] + turned
                        half //= 2
                    for side in range(2):
                        spot = 2 * step + side
                        diag_sums[head, spot : spot + 1, :] = wide[:, TILE * side : TILE * (side + 1)]
                for side in range(2):
                    diag_sums[head, 6 + side : 7 + side, :] = jnp.sum(far_sums[side], 0, keepdims=True)
            for block in range(blocks):
                piece = slice(block * TILE, (block + 1) * TILE)
                grads[0, piece, lanes] = (query_sum[block] * 0.125).astype(BF16)
            grads[1, :, lanes] = (key_sum * 0.125).astype(BF16)
            grads[2, :, lanes] = value_sum.astype(BF16)
            return carry

        lax.fori_loop(0, cols // two_heads, pair, 0)
        for c in range(3):
            weight_grad = dot_nn(norm_t[...], grads[c]).astype(BF16)

            @pl.when(group > 0)
            def _():
                wg[group - 1, c] = weight_grad

            @pl.when(group == 0)
            def _():
                total[c * width : (c + 1) * width, :] = weight_grad

            norm_grad[...] += dot_nt(grads[c], qkvw[slot, c])

    def add_into(target, *others):
        for first in range(0, target.shape[0], 256):
            spot = slice(first, first + 256)
            value = target[spot].astype(F32)
            for other in others:
                value = value + other[spot].astype(F32)
            target[spot] = value.astype(BF16)

    third = outw.shape[1]
    parts = 4
    length = total.shape[0] // parts
    stages = len(dp_bits)

    def bit_of(step):
        return lax.rem(lax.div(me, dp_bits[step]), 2)

    def segment(part, step):
        first, size_of = part * length, length
        for s in range(step):
            size_of //= 2
            first = first + bit_of(s) * size_of
        return first, size_of

    def halving(part, step):
        first, size_of = segment(part, step)
        half = size_of // 2
        away = pl.multiple_of(first + (1 - bit_of(step)) * half, half)
        return remote_copy(
            total.at[pl.ds(away, half)],
            total_got.at[pl.ds(part * length + length - size_of, half)],
            total_sems.at[part, 0, step, 0], total_sems.at[part, 0, step, 1], "dp",
            flip(me, dp_bits[step], size),
        )

    def add_half(part, step):
        first, half = segment(part, step + 1)
        first = pl.multiple_of(first, half)
        got = part * length + length - 2 * half
        value = total[pl.ds(first, half), :].astype(F32) + total_got[got : got + half, :].astype(F32)
        total[pl.ds(first, half), :] = value.astype(BF16)
        if step == stages - 1:
            sum_ref[pl.ds(first, half), :] = value.astype(BF16)

    def doubling(part, step):
        first, size_of = segment(part, step + 1)
        spot = pl.ds(pl.multiple_of(first, size_of), size_of)
        return remote_copy(
            sum_ref.at[spot], sum_ref.at[spot],
            total_sems.at[part, 1, step, 0], total_sems.at[part, 1, step, 1], "dp",
            flip(me, dp_bits[step], size),
        )

    def sum_stage(part, stage):
        if 0 < stage <= stages:
            halving(part, stage - 1).wait()
            add_half(part, stage - 1)
        elif stage > stages:
            doubling(part, 2 * stages - stage).wait()
        if stage < stages:
            halving(part, stage).start()
        elif stage < 2 * stages:
            doubling(part, 2 * stages - 1 - stage).start()

    def group_step(step, carry):
        @pl.when(step == groups - 1)
        def _():
            far_copy(1).start()

        attend_group(step)

        @pl.when(step == 0)
        def _():
            send_made(1)
            qkv_copy(0).start()
            small_step(0, early_ref, early_got, 1)
            out_copy(0).wait_recv()
            add_into(wo.at[2], wo_got.at[0])
            out_copy(2).start()

        @pl.when(step == 1)
        def _():
            send_made(2)
            qkv_copy(0).wait_recv()
            for c in range(3):
                add_into(wg.at[1, c], wg_got.at[0, c])
            qkv_copy(2).start()
            small_step(0, early_ref, early_got, 2)

        @pl.when(step == 2)
        def _():
            qkv_copy(1).start()
            small_step(0, early_ref, early_got, 3)
            out_copy(1).wait_recv()
            out_copy(2).wait_recv()
            add_into(wo.at[0], wo_got.at[1], wo_got.at[2])
            total[3 * third :, :] = wo[0]
            sum_stage(3, 0)

        return carry

    lax.fori_loop(0, groups, group_step, 0)
    sum_stage(3, 1)

    small_step(0, early_ref, early_got, 4)
    unit, recip = unit_norm(tok[...].astype(F32))
    gain_grad = jnp.sum(norm_grad[...] * unit, 0, keepdims=True)
    table_grad = 0.0
    for k in range(8):
        for piece in split_three(diag_sums[:, k, :]):
            table_grad = table_grad + dot_nt(piece.astype(BF16), ones_ref[:, k * TILE : (k + 1) * TILE])
    late_ref[0] = jnp.zeros(late_ref.shape[1:], F32)
    for k in range(width // TILE):
        late_ref[0, k : k + 1, :] = gain_grad[:, k * TILE : (k + 1) * TILE]
    heads, buckets = table_grad.shape
    late_ref[0, 8 : 8 + heads, :buckets] = table_grad
    small_step(1, late_ref, late_got, 0)

    qkv_copy(1).wait_recv()
    qkv_copy(2).wait()
    def finish_tokens():
        scaled = norm_grad[...] * gain_ref[0:1, :]
        back = recip * (scaled - unit * jnp.mean(scaled * unit, -1, keepdims=True))
        grad_ref[...] = (grad_hidden[...] + back).astype(BF16)
        hidden_again.start()
        if not remote_made:
            loads[8].start()

    def finish_output():
        loads[8].wait()
        hidden_again.wait()
        if remote_made:
            for _, peer in peers:
                made_copy(me, peer, peer).wait_recv()
        values = made[...].reshape(experts * capacity, width) if remote_made else rows[...]
        for first in range(0, count, 256):
            spot = slice(first, first + 256)
            value = hidden[spot, :]
            for k in range(2):
                hit = onehot_columns(slots[k][spot], 0, experts * capacity)
                value = value + gates[k][spot] * dot_nn(hit.astype(F32).astype(BF16), values)
            output_ref[spot, :] = value.astype(BF16)

    rest_early = list(range(groups + 1, len(exchanges) + 1))
    rest_late = list(range(1, len(exchanges) + 1))

    def next_small():
        if rest_early:
            small_step(0, early_ref, early_got, rest_early.pop(0))
        if rest_late:
            small_step(1, late_ref, late_got, rest_late.pop(0))

    for time in range(3 + 2 * stages):
        for part in range(min(3, time + 1)):
            if time == part:
                add_into(
                    total.at[part * third : (part + 1) * third], wg_got.at[1, part], wg_got.at[2, part]
                )
            if time - part <= 2 * stages:
                sum_stage(part, time - part)
        if time + 2 <= 2 * stages:
            sum_stage(3, time + 2)
        if time == 0:
            finish_tokens()
        elif time == 1:
            finish_output()
        elif time == 2:
            far_copy(1).wait()
            far_copy(2).start()
        next_small()
    while rest_early or rest_late:
        next_small()
    saves = [
        pltpu.make_async_copy(sum_ref.at[pl.ds(0, 3 * third)], sum_out, load_sems.at[10]),
        pltpu.make_async_copy(sum_ref.at[pl.ds(3 * third, third)], sum_out_two, load_sems.at[11]),
    ]
    for copy in saves:
        copy.start()
    last = len(exchanges) % 2
    router_out[...] = early_ref[last, :experts, :]
    gains_out[1:2, :] = early_ref[last, experts : experts + 1, :]
    for k in range(width // TILE):
        gains_out[0:1, k * TILE : (k + 1) * TILE] = late_ref[last, k : k + 1, :]
    table_out[...] = late_ref[last, 8 : 8 + heads, :buckets]
    for copy in saves:
        copy.wait()
    far_copy(0).wait()
    far_copy(2).wait()
    if remote_made:
        for _, peer in peers:
            made_copy(peer, me, peer).wait_send()
    for kind in range(3):
        out_copy(kind).wait_send()
    for kind in range(2):
        qkv_copy(kind).wait_send()


def bits_below(size):
    return [1 << b for b in range(size.bit_length() - 1)]


def rear(
    span, gains, table_t, ones, router_t3, slots_col, gates, extra, tokens, cotangent, hidden, normed,
    mixed, rows, made, out_weights, qkv_weights, qkv, expert_sums, head_size,
):
    count, width = tokens.shape
    size, groups = lax.axis_size("dp"), lax.axis_size("wshard")
    heads, buckets = width // head_size, ones.shape[0]
    experts = router_t3.shape[0] // 3
    cols = out_weights.shape[2]
    exchanges = len(bits_below(size)) + len(bits_below(groups))
    dma = pltpu.SemaphoreType.DMA
    wide, small = (count, width), (experts + EXTRA, width)
    late = (8 + heads, TILE)
    total = (4 * width, cols)
    vmem = pltpu.VMEM
    return pl.pallas_call(
        functools.partial(rear_body, size, groups, head_size, made.ndim == 3),
        out_shape=(
            shape_of(wide, BF16),
            shape_of(wide, BF16),
            shape_of((2, width), F32),
            shape_of((heads, buckets), F32),
            shape_of((experts, width), F32),
            shape_of((3 * width, cols), BF16),
            shape_of((width, cols), BF16),
            shape_of(expert_sums.shape[1:], BF16),
        ),
        in_specs=[SMEM] + [VMEM] * 7 + [ANY] * 11,
        out_specs=(VMEM,) * 5 + (ANY,) * 3,
        scratch_shapes=[
            vmem(wide, BF16),
            vmem(wide, BF16),
            vmem(wide, F32),
            vmem(wide, BF16),
            vmem(wide, BF16),
            vmem(rows.shape, BF16),
            vmem(made.shape if made.ndim == 3 else (16, TILE), BF16),
            vmem(out_weights.shape, BF16),
            vmem((2, *qkv_weights.shape[1:]), BF16),
            vmem(qkv.shape, BF16),
            vmem((width, count), BF16),
            vmem((count, count), F32),
            vmem(wide, F32),
            vmem((3, count, cols), BF16),
            vmem((2, count, count), BF16),
            vmem((2, count, count), BF16),
            vmem((heads, 8, TILE), F32),
            vmem((groups, width, cols), BF16),
            vmem((3, width, cols), BF16),
            vmem((groups - 1, 3, width, cols), BF16),
            vmem((3, 3, width, cols), BF16),
            vmem(total, BF16),
            vmem(total, BF16),
            vmem(total, BF16),
            vmem((2, *small), F32),
            vmem((exchanges, *small), F32),
            vmem((2, *late), F32),
            vmem((exchanges, *late), F32),
            vmem((heads, ones.shape[1]), F32),
            dma((12,)),
            dma((2,)),
            dma((size,)),
            dma((size,)),
            dma((2, 3, 2)),
            dma((4, 2, len(bits_below(size)), 2)),
            dma((2, exchanges, 2)),
            dma((3, 2)),
        ],
        cost_estimate=pl.CostEstimate(flops=LIGHT, bytes_accessed=LIGHT, transcendentals=0),
        compiler_params=pltpu.CompilerParams(
            collective_id=2, has_side_effects=True, vmem_limit_bytes=66_000_000
        ),
        name="rear",
    )(
        span, gains, table_t, ones, router_t3, slots_col, gates, extra, tokens, cotangent, hidden,
        normed, mixed, rows, made, out_weights, qkv_weights, qkv, expert_sums,
    )


def result_body(
    in_ref, far_in_ref, down_ref, far_down_ref, qkv_ref, out_ref, output_ref, tokens_ref, gains_ref,
    table_ref, router_ref,
    in_out, down_out, qkv_out, out_out, output_out, tokens_out, gains_out, table_out, router_out,
):
    for c in range(2):
        in_out[c] = in_ref[0, c].astype(F32) + far_in_ref[c].astype(F32)
    down_out[...] = down_ref[0, 0].astype(F32) + far_down_ref[0].astype(F32)
    qkv_out[...] = qkv_ref[...].astype(F32)
    out_out[...] = out_ref[...].astype(F32)
    output_out[...] = output_ref[...]
    tokens_out[...] = tokens_ref[...]
    gains_out[...] = gains_ref[...]
    table_out[...] = table_ref[...]
    router_out[...] = router_ref[...]


def results(expert_sums, far_got, qkv_sum, out_sum, output, grad_tokens, *small, steps=4):
    share, width = far_got.shape[1:]
    part = share // steps

    def rows_of(array):
        return pl.BlockSpec((array.shape[0] // steps, array.shape[1]), lambda i: (i, 0))

    def whole(array):
        return pl.BlockSpec(array.shape, lambda i: (0, 0))

    tall = (qkv_sum, out_sum, output, grad_tokens)
    return pl.pallas_call(
        result_body,
        grid=(steps,),
        out_shape=(
            shape_of((2, share, width), F32),
            shape_of((share, width), F32),
            shape_of(qkv_sum.shape, F32),
            shape_of(out_sum.shape, F32),
            shape_of(output.shape, BF16),
            shape_of(grad_tokens.shape, BF16),
        )
        + tuple(shape_of(a.shape, F32) for a in small),
        in_specs=[
            pl.BlockSpec((1, 2, part, width), lambda i: (0, 0, i, 0)),
            pl.BlockSpec((2, part, width), lambda i: (0, i, 0)),
            pl.BlockSpec((1, 1, part, width), lambda i: (0, 2, i, 0)),
            pl.BlockSpec((1, part, width), lambda i: (2, i, 0)),
        ]
        + [rows_of(a) for a in tall]
        + [whole(a) for a in small],
        out_specs=(
            pl.BlockSpec((2, part, width), lambda i: (0, i, 0)),
            pl.BlockSpec((part, width), lambda i: (i, 0)),
        )
        + tuple(rows_of(a) for a in tall)
        + tuple(whole(a) for a in small),
        cost_estimate=pl.CostEstimate(flops=LIGHT, bytes_accessed=LIGHT, transcendentals=0),
        name="results",
    )(expert_sums, far_got, expert_sums, far_got, *tall, *small)


def swap(value, axis, bit):
    size = lax.axis_size(axis)
    return lax.ppermute(value, axis, [(i, i ^ bit) for i in range(size)])


def bits_of(axis):
    size = lax.axis_size(axis)
    return [1 << b for b in range(size.bit_length() - 1)]


def after(value, *others):
    return lax.optimization_barrier((value, *others))[0]


def exchange(rows, axis):
    size = lax.axis_size(axis)
    total, width = rows.shape
    blocks = rows.reshape(size, total // size, width)
    return lax.all_to_all(blocks, axis, 0, 0, tiled=True)


def per_device(
    tokens,
    cotangent,
    span_starts,
    routes,
    norm_gains,
    bias_table,
    router,
    attn_qkv,
    attn_out,
    expert_in,
    expert_down,
):
    assert span_starts.shape[0] == 1
    tok_count, model_width = tokens.shape
    buckets, head_count = bias_table.shape
    head_size = model_width // head_count
    experts = router.shape[1]
    capacity = (10 * tok_count + 4 * experts - 1) // (4 * experts)
    total = experts * capacity
    place = lax.axis_index("wshard")
    where = jnp.stack([place.astype(I32), span_starts[0]])
    ones = jnp.asarray(diagonal_ones(buckets), BF16)
    table_t = bias_table.T
    router_t = router.T
    expert_in = jnp.swapaxes(expert_in[0], 1, 2)
    expert_down = expert_down[0]

    shards = (attn_qkv, attn_out, expert_in)
    (
        slots_col, gates, sent_gates, qkv_all, out_all, qkv, mixed, hidden, normed_two, sent,
        outer_rows, far_gate,
    ) = front(
        span_starts, routes, norm_gains, table_t, ones, router_t, tokens, cotangent, shards, head_size,
        capacity,
    )
    groups = out_all.shape[0]
    through = moe if capacity % 16 == 0 else moe_plain
    back_rows, back_extra, made, expert_grads = through(
        sent, sent_gates, outer_rows, expert_in, expert_down, far_gate
    )
    if through is moe_plain:
        made = exchange(made.reshape(total, model_width), "dp").reshape(total, model_width)

    output, grad_tokens, grad_gains, table_grad, router_grad, qkv_sum, out_sum, far_got = rear(
        span_starts, norm_gains, table_t, ones, jnp.concatenate([router_t] * 3, 0),
        slots_col, gates, back_extra, tokens, cotangent, hidden, normed_two,
        mixed, back_rows.reshape(total, model_width), made, out_all, qkv_all, qkv, expert_grads,
        head_size,
    )

    (
        in_grad, down_grad, qkv_sum, out_sum, output, grad_tokens, grad_gains, table_grad, router_grad,
    ) = results(
        expert_grads, far_got, qkv_sum, out_sum, output, grad_tokens, grad_gains, table_grad,
        router_grad,
    )
    return (
        output,
        grad_tokens,
        grad_gains,
        table_grad.T,
        router_grad.T,
        qkv_sum.reshape(3, model_width, out_sum.shape[1]),
        out_sum,
        jnp.swapaxes(in_grad, 1, 2)[None],
        down_grad[None],
    )


def solution(mesh):
    return jax.shard_map(
        per_device,
        mesh=mesh,
        in_specs=(
            P(("dp", "wshard"), None),
            P(("dp", "wshard"), None),
            P(("dp", "wshard")),
            P(("dp", "wshard"), None),
            P(),
            P(),
            P(),
            P(None, None, "wshard"),
            P(None, "wshard"),
            P("dp", None, None, "wshard"),
            P("dp", "wshard", None),
        ),
        out_specs=(
            P(("dp", "wshard"), None),
            P(("dp", "wshard"), None),
            P(),
            P(),
            P(),
            P(None, None, "wshard"),
            P(None, "wshard"),
            P("dp", None, None, "wshard"),
            P("dp", "wshard", None),
        ),
        check_vma=False,
    )
```

profile of v0, /device:TPU:0, one launch (start us, length us, event | category | flops | bytes accessed | tf_op | source)
XLA Modules:
  0.0 409.6 jit_solution(7486879704981214620)
XLA Ops:
  1.3 74.6 %front.1 = (s32[512,8]{1,0:T(8,128)}, f32[512,2]{1,0:T(8,128)}, f32[8,8,256]{2,1,0:T(8,128)}, bf16[4,3,1024,256]{3,2,1,0:T(8,128)(2,1)}, bf16[4,1024,256]{2,1,0:...) custom-call(s32[1]{0:T(128)S(6)} %copy.21.span_ref, ...), custom_call_target="tpu_custom_call" | custom-call | flops 1024 | bytes 1024 | tf_op jit(solution)/shard_map/front/pallas_call | solution.py:404
  75.9 0.0 copy-start
  75.9 159.5 %experts.1 = (bf16[8,160,1024]{2,1,0:T(8,128)(2,1)}, f32[8,8,256]{2,1,0:T(8,128)}, bf16[8,160,1024]{2,1,0:T(8,128)(2,1)}, bf16[2,3,704,1024]{3,2,1,0:T(8,128)(2,1)}, bf16[2,3,704,1024]{3,2,1,0:T(8,128)(2,1)}) custom-call(bf16[8,160,1024]{2,1,0:T(8,128)(2,1)} %get-tuple-element.42.sent_ref, f32[8,8,256]{2,1,0:T(8,128)} %get-tuple-element.43.gates_ref, ...), custom_call_target="tpu_custom_call" | custom-call | flops 1024 | bytes 1024 | tf_op jit(solution)/shard_map/experts/pallas_call | solution.py:793
  235.5 0.0 copy-done
  235.5 0.6 pad_maximum_fusion.router_ref
  236.1 163.4 %rear.1 = (bf16[512,1024]{1,0:T(8,128)(2,1)}, bf16[512,1024]{1,0:T(8,128)(2,1)}, f32[2,1024]{1,0:T(2,128)}, f32[16,32]{1,0:T(8,128)}, f32[8,1024]{1,0:T(8,128)},...) custom-call(s32[1]{0:T(128)S(6)} %copy.21.span_ref, f32[2,1024]{1,0:T(2,128)} %gain_ref.3, ...), custom_call_target="tpu_custom_call" | custom-call | flops 1024 | bytes 1024 | tf_op jit(solution)/shard_map/rear/pallas_call | solution.py:1415
  399.5 9.9 %results.1 = (f32[2,704,1024]{2,1,0:T(8,128)}, f32[704,1024]{1,0:T(8,128)}, f32[3072,256]{1,0:T(8,128)}, f32[1024,256]{1,0:T(8,128)}, bf16[512,1024]{1,0:T(8,128...) custom-call(bf16[2,3,704,1024]{3,2,1,0:T(8,128)(2,1)} %get-tuple-element.46.far_hb, ...), custom_call_target="tpu_custom_call" | custom-call | flops 1024 | bytes 1024 | tf_op jit(solution)/shard_map/results/pallas_call | solution.py:1507
Async XLA Ops:
  75.9 159.5 %copy-start = (bf16[1024,8]{0,1:T(8,128)(2,1)S(1)}, bf16[1024,8]{0,1:T(8,128)(2,1)}, u32[]{:S(2)}) copy-start(bf16[1024,8]{0,1:T(8,128)(2,1)} %param.18) | copy-start | bytes 49156
where the time goes:
time: 414 us; the launch traced here: 410 us
  Pallas kernels  407 us (98%)
    pallas_call x1, Pallas kernels, rear(): pl.pallas_call(functools.partial(rear_body, size, groups, head_size, made...  163 us
    pallas_call x1, Pallas kernels, moe(): pl.pallas_call(functools.partial(moe_body, size, groups, chunk), out_shap...  160 us
    pallas_call x1, Pallas kernels, front(): pl.pallas_call(functools.partial(front_body, size, groups, head_size), ou...  74.6 us
    pallas_call x1, Pallas kernels, results(): pl.pallas_call(result_body, grid=(steps,), out_shape=(shape_of((2, share,...  9.93 us

commit v1 on v0

--- a/solution.py
+++ b/solution.py
@@ -1493,7 +1493,7 @@
     router_out[...] = router_ref[...]
 
 
-def results(expert_sums, far_got, qkv_sum, out_sum, output, grad_tokens, *small, steps=4):
+def results(expert_sums, far_got, qkv_sum, out_sum, output, grad_tokens, *small, steps=2):
     share, width = far_got.shape[1:]
     part = share // steps
 

time: 414 us -> 413 us (level)
  no operation moved by 1% of the time
where the time goes in v1:
time: 413 us; the launch traced here: 409 us
  Pallas kernels  407 us (99%)
    pallas_call x1, Pallas kernels, rear(): pl.pallas_call(functools.partial(rear_body, size, groups, head_size, made...  163 us
    pallas_call x1, Pallas kernels, moe(): pl.pallas_call(functools.partial(moe_body, size, groups, chunk), out_shap...  160 us
    pallas_call x1, Pallas kernels, front(): pl.pallas_call(functools.partial(front_body, size, groups, head_size), ou...  74.6 us
    pallas_call x1, Pallas kernels, results(): pl.pallas_call(result_body, grid=(steps,), out_shape=(shape_of((2, share,...  9.01 us

profile of v1, /device:TPU:0, one launch (start us, length us, event | category | flops | bytes accessed | tf_op | source)
XLA Modules:
  0.0 408.7 jit_solution(7809167442362878540)
XLA Ops:
  1.3 74.6 %front.1 = (s32[512,8]{1,0:T(8,128)}, f32[512,2]{1,0:T(8,128)}, f32[8,8,256]{2,1,0:T(8,128)}, bf16[4,3,1024,256]{3,2,1,0:T(8,128)(2,1)}, bf16[4,1024,256]{2,1,0:...) custom-call(s32[1]{0:T(128)S(6)} %copy.21.span_ref, ...), custom_call_target="tpu_custom_call" | custom-call | flops 1024 | bytes 1024 | tf_op jit(solution)/shard_map/front/pallas_call | solution.py:404
  75.9 0.0 copy-start
  75.9 159.5 %experts.1 = (bf16[8,160,1024]{2,1,0:T(8,128)(2,1)}, f32[8,8,256]{2,1,0:T(8,128)}, bf16[8,160,1024]{2,1,0:T(8,128)(2,1)}, bf16[2,3,704,1024]{3,2,1,0:T(8,128)(2,1)}, bf16[2,3,704,1024]{3,2,1,0:T(8,128)(2,1)}) custom-call(bf16[8,160,1024]{2,1,0:T(8,128)(2,1)} %get-tuple-element.42.sent_ref, f32[8,8,256]{2,1,0:T(8,128)} %get-tuple-element.43.gates_ref, ...), custom_call_target="tpu_custom_call" | custom-call | flops 1024 | bytes 1024 | tf_op jit(solution)/shard_map/experts/pallas_call | solution.py:793
  235.5 0.0 copy-done
  235.5 0.6 pad_maximum_fusion.router_ref
  236.1 163.4 %rear.1 = (bf16[512,1024]{1,0:T(8,128)(2,1)}, bf16[512,1024]{1,0:T(8,128)(2,1)}, f32[2,1024]{1,0:T(2,128)}, f32[16,32]{1,0:T(8,128)}, f32[8,1024]{1,0:T(8,128)},...) custom-call(s32[1]{0:T(128)S(6)} %copy.21.span_ref, f32[2,1024]{1,0:T(2,128)} %gain_ref.3, ...), custom_call_target="tpu_custom_call" | custom-call | flops 1024 | bytes 1024 | tf_op jit(solution)/shard_map/rear/pallas_call | solution.py:1415
  399.5 9.0 %results.1 = (f32[2,704,1024]{2,1,0:T(8,128)}, f32[704,1024]{1,0:T(8,128)}, f32[3072,256]{1,0:T(8,128)}, f32[1024,256]{1,0:T(8,128)}, bf16[512,1024]{1,0:T(8,128...) custom-call(bf16[2,3,704,1024]{3,2,1,0:T(8,128)(2,1)} %get-tuple-element.46.far_hb, ...), custom_call_target="tpu_custom_call" | custom-call | flops 1024 | bytes 1024 | tf_op jit(solution)/shard_map/results/pallas_call | solution.py:1507
Async XLA Ops:
  75.9 159.5 %copy-start = (bf16[1024,8]{0,1:T(8,128)(2,1)S(1)}, bf16[1024,8]{0,1:T(8,128)(2,1)}, u32[]{:S(2)}) copy-start(bf16[1024,8]{0,1:T(8,128)(2,1)} %param.18) | copy-start | bytes 49156
